TPU v7x, 32 devices: a whole 2x2x4 slice. The times are simulated.
32 devices in a mesh: groups: 2 (over x), region: 16 (over z, y, core).
Axes of the slice: x: 2, y: 2, z: 4, core: 2. Of those that a mesh axis runs over, the one named last changes fastest.
Arguments:
- record: bfloat16 [16384, 640], P(('groups', 'region')), parts along dimension 0, may hold values from -6 to 6
- target: bfloat16 [4, 16384, 8192], P(None, ('groups', 'region')), parts along dimension 1, may hold values from -0.59765625 to 0.59765625
- offset: int32 [2], P('groups'), parts along dimension 0, may hold values from 0 to 127
- lag_steps: int32 [6], P('groups'), parts along dimension 0, may hold values from 1 to 8
Outputs:
- grad: float32 [16384, 640], P(('groups', 'region')), parts along dimension 0
There are 2 independent parts, one for each index of `groups`. A program takes and returns all parts, laid end to end along the dimension named above; each array names one. Nothing has to cross between parts.
All inputs are finite; a program needn't handle non-finite values.
Results may differ from a plain program's by a relative error of at most 0.0005.
Values may be sent and summed in bfloat16 or wider, within the bound.
A program may use at most 256 MiB of HBM per device.

v0:
```python
import jax
import jax.numpy as jnp
from jax import lax
from jax.sharding import PartitionSpec as P

REGIONS = 8192
SAMPLES = 384
SLACK = 128
LAGS = 3


def shifted(value, axis, steps):
    count = lax.axis_size(axis)
    pairs = [(source, (source + steps) % count) for source in range(count)]
    return lax.ppermute(value, axis, pairs)


def outer_dot(left, right):
    return lax.dot_general(
        left, right, (((1,), (1,)), ((), ())), preferred_element_type=jnp.float32
    )


def split_views(window, lag_steps):
    early_view = window[:, :SAMPLES]
    later_list = []
    for lag_number in range(LAGS):
        later_list.append(lax.dynamic_slice_in_dim(window, lag_steps[lag_number], SAMPLES, 1))
    return (early_view, jnp.stack(later_list))


def place_views(early_part, later_parts, lag_steps, win_width):
    block_rows = early_part.shape[0]
    placed = jnp.pad(early_part, ((0, 0), (0, win_width - SAMPLES)))
    blank = jnp.zeros((block_rows, win_width), jnp.float32)
    for lag_number in range(LAGS):
        placed = placed + lax.dynamic_update_slice(
            blank, later_parts[lag_number], (0, lag_steps[lag_number])
        )
    return placed


def pair_tiles(own_views, other_views, target, flipped, column_at, width, factor):
    inverse = 1.0 / SAMPLES
    weight = SAMPLES / REGIONS
    own_early, own_later = own_views
    other_early, other_later = other_views
    tiles = lax.dynamic_slice_in_dim(target, column_at, width, 2).astype(jnp.float32)
    mirror = lax.dynamic_slice_in_dim(flipped, column_at, width, 2).astype(jnp.float32)
    cov_zero = outer_dot(own_early, other_early) * inverse
    cov_fore = (
        jnp.einsum("rs,lcs->lrc", own_early, other_later, preferred_element_type=jnp.float32)
        * inverse
    )
    cov_back = (
        jnp.einsum("lrs,cs->lrc", own_later, other_early, preferred_element_type=jnp.float32)
        * inverse
    )
    sym_err = (weight * (2.0 * cov_zero - tiles[0] - mirror[0]) * factor).astype(jnp.bfloat16)
    fore_err = (weight * (cov_fore - tiles[1:]) * factor).astype(jnp.bfloat16)
    back_err = (weight * (cov_back - mirror[1:]) * factor).astype(jnp.bfloat16)
    return (sym_err, fore_err, back_err)


def own_terms(errors, other_views):
    sym_err, fore_err, back_err = errors
    other_early, other_later = other_views
    to_early = jnp.dot(sym_err, other_early, preferred_element_type=jnp.float32)
    to_early = to_early + jnp.einsum(
        "lrc,lcs->rs", fore_err, other_later, preferred_element_type=jnp.float32
    )
    to_later = jnp.einsum("lrc,cs->lrs", back_err, other_early, preferred_element_type=jnp.float32)
    return (to_early, to_later)


def other_terms(errors, own_views):
    sym_err, fore_err, back_err = errors
    own_early, own_later = own_views
    to_early = jnp.einsum("rc,rs->cs", sym_err, own_early, preferred_element_type=jnp.float32)
    to_early = to_early + jnp.einsum(
        "lrc,lrs->cs", back_err, own_later, preferred_element_type=jnp.float32
    )
    to_later = jnp.einsum("lrc,rs->lcs", fore_err, own_early, preferred_element_type=jnp.float32)
    return (to_early, to_later)


def shards(record, target, offset, lag_steps):
    block_rows = record.shape[0]
    begin_at = offset[0]
    win_width = SAMPLES + SLACK
    window = lax.dynamic_slice_in_dim(record, begin_at, win_width, 1)
    own_views = split_views(window, lag_steps)
    devices = lax.axis_size("region")
    own_index = lax.axis_index("region")
    stacked = target.shape[0]
    received = lax.all_to_all(target, "region", split_axis=2, concat_axis=2, tiled=True)
    flipped = (
        received.reshape(stacked, block_rows, devices, block_rows)
        .transpose(0, 3, 2, 1)
        .reshape(stacked, block_rows, devices * block_rows)
    )
    errors = pair_tiles(
        own_views, own_views, target, flipped, own_index * block_rows, block_rows, 1.0
    )
    grad_early, grad_later = own_terms(errors, own_views)
    halfway = devices // 2

    def visit_block(step_number, loop_state):
        visitor, partials, grad_early, grad_later = loop_state
        visitor = shifted(visitor, "region", 1)
        partials = shifted(partials, "region", 1)
        block_id = (own_index - step_number + devices) % devices
        factor = jnp.where(step_number == halfway, 0.5, 1.0)
        other_views = split_views(visitor, lag_steps)
        errors = pair_tiles(
            own_views, other_views, target, flipped, block_id * block_rows, block_rows, factor
        )
        add_early, add_later = own_terms(errors, other_views)
        to_early, to_later = other_terms(errors, own_views)
        partials = partials + place_views(to_early, to_later, lag_steps, win_width)
        return (visitor, partials, grad_early + add_early, grad_later + add_later)

    def visit_four(turn_number, loop_state):
        for inner in range(4):
            loop_state = visit_block(1 + 4 * turn_number + inner, loop_state)
        return loop_state

    start_state = (window, jnp.zeros((block_rows, win_width), jnp.float32), grad_early, grad_later)
    final_state = lax.fori_loop(0, halfway // 4, visit_four, start_state)
    returned = shifted(final_state[1], "region", halfway)
    in_window = place_views(final_state[2], final_state[3], lag_steps, win_width) + returned
    grad = lax.dynamic_update_slice(jnp.zeros(record.shape, jnp.float32), in_window, (0, begin_at))
    return grad


def solution(mesh):
    placed = (
        P(("groups", "region"), None),
        P(None, ("groups", "region"), None),
        P("groups"),
        P("groups"),
    )
    return jax.shard_map(
        shards, mesh=mesh, in_specs=placed, out_specs=P(("groups", "region"), None), check_vma=False
    )
```

profile of v0, /device:TPU:0, one launch (start us, length us, event | category | flops | bytes accessed | tf_op | source)
XLA Modules:
  0.0 1366.3 jit_solution(1209809443540427602)
XLA Ops:
  0.0 54.7 %copy.41 = bf16[4,512,8192]{1,0,2:T(4,128)(2,1)} copy(bf16[4,512,8192]{2,1,0:T(8,128)(2,1)} %param.7) | data formatting | bytes 67108864 | tf_op args[1]
  54.7 7.6 all-to-all-start
  82.9 568.3 %all-to-all-done = bf16[4,512,8192]{1,0,2:T(4,128)(2,1)} async-done(((bf16[4,512,8192]{1,0,2:T(4,128)(2,1)}), bf16[4,512,8192]{1,0,2:T(4,128)(2,1)}, u32[]{:S(2)}, u32[]{:S(2)}) %all-to-all-start) | async-done | bytes 33554464 | tf_op jit(solution)/shard_map/all_to_all | solution.py:96
  651.2 31.1 %copy.58 = bf16[4,512,16,512]{1,2,3,0:T(8,128)(2,1)} copy(bf16[4,512,16,512]{1,0,3,2:T(4,128)(2,1)} %bitcast.2) | data formatting | bytes 67108864 | tf_op jit(solution)/shard_map/reshape | solution.py:98
  682.3 50.0 %reshape.7 = bf16[4,512,8192]{2,1,0:T(8,128)(2,1)} reshape(bf16[4,512,16,512]{3,2,1,0:T(8,128)(2,1)} %bitcast.439) | data formatting | bytes 67108864 | tf_op jit(solution)/shard_map/reshape | solution.py:100
  742.2 569.7 %while.23 = (s32[]{:T(128)}, bf16[512,512]{1,0:T(8,128)(2,1)S(1)}, f32[512,512]{1,0:T(8,128)}, f32[512,384]{1,0:T(8,128)}, f32[3,512,384]{2,1,0:T(8,128)}, /*ind...) while((s32[]{:T(128)}, bf16[512,512]{1,0:T(8,128)(2,1)S(1)}, ...), condition=%wide.region_1.2_spmd.clone, body=%wide.region_0.1_spmd.clone.sunk | while | flops 16968056832 | bytes 541067456 | solution.py:129
  744.3 44.9 %collective-permute-start.4 = (f32[512,512]{1,0:T(8,128)}, f32[512,512]{1,0:T(8,128)}, u32[]{:S(2)}, u32[]{:S(2)}) collective-permute-start(f32[512,512]{1,0:T(8,128)} %broadcast_select_fusion.2), channel_id=1, source_target_pairs={{0,1},{1,2},{2,3},{3,4},{4,5},{5,6},{6,7},{7,8},{8,9},{9,10},{10,1... | collective-permute-start | bytes 3145736 | tf_op jit(solution)/shard_map/while/body/eval_jaxpr/ppermute | solution.py:15
  789.2 15.5 %dynamic-slice_convert_fusion.11 = (f32[4,512,512]{2,1,0:T(8,128)}, f32[4,512,512]{2,1,0:T(8,128)}, f32[4,512,512]{2,1,0:T(8,128)}, f32[4,512,512]{2,1,0:T(8,128...) fusion(bf16[4,512,8192]{2,1,0:T(8,128)(2,1)} %get-tuple-element, ...), kind=kLoop, calls=%fused_computation.25.clone.1 | loop fusion | flops 8388608 | bytes 50331664 | tf_op jit(solution)/shard_map/while/body/eval_jaxpr/convert_element_type | solution.py:49
  804.7 80.8 %collective-permute-done = bf16[512,512]{1,0:T(8,128)(2,1)S(1)} collective-permute-done((bf16[512,512]{1,0:T(8,128)(2,1)S(1)}, bf16[512,512]{1,0:T(8,128)(2,1)S(1)}, u32[]{:S(2)}, u32[]{:S(2)}) %collective-permute-start) | collective-permute-done | bytes 524320 | tf_op jit(solution)/shard_map/while/body/eval_jaxpr/ppermute | solution.py:15
  896.0 3.6 copy.60
  899.6 3.7 fusion.327
  910.2 5.2 add.905
  918.0 5.2 add.906
  925.9 5.2 add.907
  936.7 11.3 collective-permute-done.1
  961.3 5.2 add.909
  969.2 5.2 add.910
  977.0 5.2 add.911
  988.1 5.9 collective-permute-done.2
  1006.4 5.2 add.913
  1014.2 5.2 add.914
  1022.1 5.2 add.915
  1048.9 6.5 add.917
  1057.7 6.5 add.918
  1072.5 6.5 add.919
  1082.0 6.1 add_add_fusion.2
  1093.6 15.5 %dynamic-slice_convert_fusion.11 = (f32[4,512,512]{2,1,0:T(8,128)}, f32[4,512,512]{2,1,0:T(8,128)}, f32[4,512,512]{2,1,0:T(8,128)}, f32[4,512,512]{2,1,0:T(8,128...) fusion(bf16[4,512,8192]{2,1,0:T(8,128)(2,1)} %get-tuple-element, ...), kind=kLoop, calls=%fused_computation.25.clone.1 | loop fusion | flops 8388608 | bytes 50331664 | tf_op jit(solution)/shard_map/while/body/eval_jaxpr/convert_element_type | solution.py:49
  1123.1 3.7 fusion.327
  1133.8 5.2 add.905
  1141.6 5.2 add.906
  1149.5 5.2 add.907
  1160.4 6.0 collective-permute-done.1
  1179.7 5.2 add.909
  1187.6 5.2 add.910
  1195.4 5.2 add.911
  1206.0 6.1 collective-permute-done.2
  1224.5 5.2 add.913
  1232.4 5.2 add.914
  1240.2 5.2 add.915
  1267.0 6.5 add.917
  1275.8 6.5 add.918
  1290.6 6.5 add.919
  1300.1 6.1 add_add_fusion.2
  1314.8 6.9 add.709
  1323.1 6.9 add.711
  1331.4 6.9 add.713
  1338.3 18.9 %collective-permute-done.8 = f32[512,512]{1,0:T(8,128)} collective-permute-done((f32[512,512]{1,0:T(8,128)}, f32[512,512]{1,0:T(8,128)}, u32[]{:S(2)}, u32[]{:S(2)}) %collective-permute-start.8) | collective-permute-done | bytes 1048608 | tf_op jit(solution)/shard_map/ppermute | solution.py:15
  1359.8 6.1 dynamic_update_slice.75
  (290 shorter events, 255.8 us)
Async XLA Ops:
  54.7 7.6 copy-start.34
  54.7 14.5 %copy-start.32 = (bf16[512,640]{1,0:T(8,128)(2,1)S(1)}, bf16[512,640]{1,0:T(8,128)(2,1)}, u32[]{:S(2)}) copy-start(bf16[512,640]{1,0:T(8,128)(2,1)} %param.6) | copy-start | bytes 1966084
  54.7 596.5 %all-to-all-start = ((bf16[4,512,8192]{1,0,2:T(4,128)(2,1)}), bf16[4,512,8192]{1,0,2:T(4,128)(2,1)}, u32[]{:S(2)}, u32[]{:S(2)}) async-start(bf16[4,512,8192]{1,0,2:T(4,128)(2,1)} %copy.41), calls=%async_computation | async-start | bytes 67108864 | tf_op jit(solution)/shard_map/all_to_all | solution.py:96
  76.6 4.3 copy-start.25
  732.2 4.4 copy-start.27
  742.4 143.1 %collective-permute-start = (bf16[512,512]{1,0:T(8,128)(2,1)S(1)}, bf16[512,512]{1,0:T(8,128)(2,1)S(1)}, u32[]{:S(2)}, u32[]{:S(2)}) collective-permute-start(bf16[512,512]{1,0:T(8,128)(2,1)S(1)} %get-tuple-element.604), channel_id=1, source_target_pairs={{0,1},{1,2},{2,3},{3,4},{4,5},{5,6},{6,7},{7,8},{8,9},{9,10},{10,1... | collective-permute-start | bytes 1572872 | tf_op jit(solution)/shard_map/while/body/eval_jaxpr/ppermute | solution.py:15
  744.3 208.1 %collective-permute-start.4 = (f32[512,512]{1,0:T(8,128)}, f32[512,512]{1,0:T(8,128)}, u32[]{:S(2)}, u32[]{:S(2)}) collective-permute-start(f32[512,512]{1,0:T(8,128)} %broadcast_select_fusion.2), channel_id=1, source_target_pairs={{0,1},{1,2},{2,3},{3,4},{4,5},{5,6},{6,7},{7,8},{8,9},{9,10},{10,1... | collective-permute-start | bytes 3145736 | tf_op jit(solution)/shard_map/while/body/eval_jaxpr/ppermute | solution.py:15
  903.2 3.1 copy-start.16
  931.1 3.1 copy-start.17
  931.1 16.8 %collective-permute-start.1 = (bf16[512,512]{1,0:T(8,128)(2,1)S(1)}, bf16[512,512]{1,0:T(8,128)(2,1)S(1)}, u32[]{:S(2)}, u32[]{:S(2)}) collective-permute-start(bf16[512,512]{1,0:T(8,128)(2,1)S(1)} %collective-permute-done), channel_id=1, source_target_pairs={{0,1},{1,2},{2,3},{3,4},{4,5},{5,6},{6,7},{7,8},{8,9},{9,10},{10,1... | collective-permute-start | bytes 1572872 | tf_op jit(solution)/shard_map/while/body/eval_jaxpr/ppermute | solution.py:15
  934.2 14.2 %copy-start.11 = (f32[4,512,512]{2,1,0:T(8,128)S(1)}, f32[4,512,512]{2,1,0:T(8,128)}, u32[]{:S(2)}) copy-start(f32[4,512,512]{2,1,0:T(8,128)} %get-tuple-element.562) | copy-start | bytes 12582916 | tf_op jit(solution)/shard_map/while
  949.5 2.9 copy-start.4
  951.4 4.5 copy-start.2
  952.4 7.7 copy-start.5
  955.9 77.9 %collective-permute-start.5 = (f32[512,512]{1,0:T(8,128)}, f32[512,512]{1,0:T(8,128)}, u32[]{:S(2)}, u32[]{:S(2)}) collective-permute-start(f32[512,512]{1,0:T(8,128)} %add.908), channel_id=1, source_target_pairs={{0,1},{1,2},{2,3},{3,4},{4,5},{5,6},{6,7},{7,8},{8,9},{9,10},{10,1... | collective-permute-start | bytes 3145736 | tf_op jit(solution)/shard_map/while/body/eval_jaxpr/ppermute | solution.py:15
  982.2 3.5 copy-start.15
  982.2 11.7 collective-permute-start.2
  985.7 8.3 copy-start.1
  995.0 3.3 copy-start.12
  1027.3 11.3 collective-permute-start.3
  1031.4 7.2 copy-start
  1036.5 31.3 %collective-permute-start.6 = (f32[512,512]{1,0:T(8,128)}, f32[512,512]{1,0:T(8,128)}, u32[]{:S(2)}, u32[]{:S(2)}) collective-permute-start(f32[512,512]{1,0:T(8,128)} %add.912), channel_id=1, source_target_pairs={{0,1},{1,2},{2,3},{3,4},{4,5},{5,6},{6,7},{7,8},{8,9},{9,10},{10,1... | collective-permute-start | bytes 3145736 | tf_op jit(solution)/shard_map/while/body/eval_jaxpr/ppermute | solution.py:15
  1039.7 3.3 copy-start.18
  1064.2 3.6 copy-start.3
  1070.2 17.9 %collective-permute-start.7 = (f32[512,512]{1,0:T(8,128)}, f32[512,512]{1,0:T(8,128)}, u32[]{:S(2)}, u32[]{:S(2)}) collective-permute-start(f32[512,512]{1,0:T(8,128)} %add.916), channel_id=1, source_target_pairs={{0,1},{1,2},{2,3},{3,4},{4,5},{5,6},{6,7},{7,8},{8,9},{9,10},{10,1... | collective-permute-start | bytes 3145736 | tf_op jit(solution)/shard_map/while/body/eval_jaxpr/ppermute | solution.py:15
  1079.0 3.0 copy-start.8
  1090.7 18.3 %collective-permute-start = (bf16[512,512]{1,0:T(8,128)(2,1)S(1)}, bf16[512,512]{1,0:T(8,128)(2,1)S(1)}, u32[]{:S(2)}, u32[]{:S(2)}) collective-permute-start(bf16[512,512]{1,0:T(8,128)(2,1)S(1)} %get-tuple-element.604), channel_id=1, source_target_pairs={{0,1},{1,2},{2,3},{3,4},{4,5},{5,6},{6,7},{7,8},{8,9},{9,10},{10,1... | collective-permute-start | bytes 1572872 | tf_op jit(solution)/shard_map/while/body/eval_jaxpr/ppermute | solution.py:15
  1093.5 77.4 %collective-permute-start.4 = (f32[512,512]{1,0:T(8,128)}, f32[512,512]{1,0:T(8,128)}, u32[]{:S(2)}, u32[]{:S(2)}) collective-permute-start(f32[512,512]{1,0:T(8,128)} %broadcast_select_fusion.2), channel_id=1, source_target_pairs={{0,1},{1,2},{2,3},{3,4},{4,5},{5,6},{6,7},{7,8},{8,9},{9,10},{10,1... | collective-permute-start | bytes 3145736 | tf_op jit(solution)/shard_map/while/body/eval_jaxpr/ppermute | solution.py:15
  1126.8 3.1 copy-start.16
  1154.7 3.3 copy-start.17
  1154.7 11.7 collective-permute-start.1
  1158.0 8.9 copy-start.11
  1168.0 2.9 copy-start.4
  1169.9 4.5 copy-start.2
  1170.9 7.7 copy-start.5
  1174.4 77.6 %collective-permute-start.5 = (f32[512,512]{1,0:T(8,128)}, f32[512,512]{1,0:T(8,128)}, u32[]{:S(2)}, u32[]{:S(2)}) collective-permute-start(f32[512,512]{1,0:T(8,128)} %add.908), channel_id=1, source_target_pairs={{0,1},{1,2},{2,3},{3,4},{4,5},{5,6},{6,7},{7,8},{8,9},{9,10},{10,1... | collective-permute-start | bytes 3145736 | tf_op jit(solution)/shard_map/while/body/eval_jaxpr/ppermute | solution.py:15
  1200.6 3.0 copy-start.15
  1200.6 11.5 collective-permute-start.2
  1203.7 8.4 copy-start.1
  1213.2 3.3 copy-start.12
  1245.5 11.3 collective-permute-start.3
  1249.5 7.2 copy-start
  1254.7 31.3 %collective-permute-start.6 = (f32[512,512]{1,0:T(8,128)}, f32[512,512]{1,0:T(8,128)}, u32[]{:S(2)}, u32[]{:S(2)}) collective-permute-start(f32[512,512]{1,0:T(8,128)} %add.912), channel_id=1, source_target_pairs={{0,1},{1,2},{2,3},{3,4},{4,5},{5,6},{6,7},{7,8},{8,9},{9,10},{10,1... | collective-permute-start | bytes 3145736 | tf_op jit(solution)/shard_map/while/body/eval_jaxpr/ppermute | solution.py:15
  1257.8 3.3 copy-start.18
  1282.4 3.6 copy-start.3
  1288.3 17.9 %collective-permute-start.7 = (f32[512,512]{1,0:T(8,128)}, f32[512,512]{1,0:T(8,128)}, u32[]{:S(2)}, u32[]{:S(2)}) collective-permute-start(f32[512,512]{1,0:T(8,128)} %add.916), channel_id=1, source_target_pairs={{0,1},{1,2},{2,3},{3,4},{4,5},{5,6},{6,7},{7,8},{8,9},{9,10},{10,1... | collective-permute-start | bytes 3145736 | tf_op jit(solution)/shard_map/while/body/eval_jaxpr/ppermute | solution.py:15
  1297.1 3.0 copy-start.8
  1312.0 45.2 %collective-permute-start.8 = (f32[512,512]{1,0:T(8,128)}, f32[512,512]{1,0:T(8,128)}, u32[]{:S(2)}, u32[]{:S(2)}) collective-permute-start(f32[512,512]{1,0:T(8,128)} %get-tuple-element.357), channel_id=1, source_target_pairs={{0,8},{1,9},{2,10},{3,11},{4,12},{5,13},{6,14},{7,15},{8,0},{9,1},... | collective-permute-start | bytes 3145736 | tf_op jit(solution)/shard_map/ppermute | solution.py:15
  (32 other events, 51.4 us)
where the time goes:
time: 1380 us; the launch traced here: 1370 us
  waiting for transfers between devices  701 us (51%)
  local copies, waits for them, and re-layouts  341 us (25%)
  matrix products  130 us (9%)
  other arithmetic  127 us (9%)
  starting transfers between devices  55.9 us (4%)
    all_to_all x1, waiting for transfers between devices, shards(): lax.all_to_all(target, 'region', split_axis=2, concat_axis=2, tiled=True)  568 us
    add x27, local copies, waits for them, and re-layouts, place_views(): placed + lax.dynamic_update_slice(blank, later_parts[lag_number], (0, lag...  153 us
    ppermute x17, waiting for transfers between devices, shifted(): return lax.ppermute(value, axis, pairs)  133 us
    unnamed x17, local copies, waits for them, and re-layouts  58.8 us
    dynamic_update_slice x27, other arithmetic, place_views(): lax.dynamic_update_slice(blank, later_parts[lag_number], (0, lag_steps[la...  56.8 us
    reshape x1, local copies, waits for them, and re-layouts, shards(): flipped = received.reshape(stacked, block_rows, devices, block_rows).tran...  50 us
    ppermute x17, starting transfers between devices, shifted(): return lax.ppermute(value, axis, pairs)  48.3 us
    convert_element_type x3, other arithmetic, pair_tiles(): lax.dynamic_slice_in_dim(flipped, column_at, width, 2).astype(jnp.float32)  33.3 us
  transfers between devices with their start and end apart: 18, of which 9 were waited for; matrix products, arithmetic and copies ran while one was open for 30% of the time, Pallas kernels for 0%

commit v1 on v0

v1 whole, which is shorter than its diff:
```python
import jax
import jax.numpy as jnp
from jax import lax
from jax.experimental import pallas as pl
from jax.experimental.pallas import tpu as pltpu
from jax.sharding import PartitionSpec as P

SAMPLES = 384
MAXLAG = 8
LAGS = 3
TERMS = 1 + LAGS
WIDE = 400
SPAN = SAMPLES + MAXLAG
WIDTH = 512


def placed_early(early, lag_steps):
    rows = early.shape[0]
    shifts = jnp.concatenate([jnp.zeros((1,), jnp.int32), lag_steps])
    padded = jnp.pad(early, ((0, 0), (MAXLAG, WIDE - SAMPLES)))
    parts = [
        lax.dynamic_slice(padded, (0, MAXLAG - shifts[term]), (rows, WIDE)) for term in range(TERMS)
    ]
    return jnp.stack(parts), shifts


def block_kernel(weight, scaled_ref, flat_ref, window_ref, target_ref, partial_ref, own_ref):
    rows = target_ref.shape[1]

    @pl.when(pl.program_id(0) == 0)
    def _():
        own_ref[...] = jnp.zeros_like(own_ref)

    window = window_ref[0]
    total = None
    for term in range(TERMS):
        cov = jnp.dot(scaled_ref[term], window, preferred_element_type=jnp.float32)
        error = (cov - weight * target_ref[term].astype(jnp.float32)).astype(jnp.bfloat16)
        own_ref[term] += lax.dot_general(
            window, error, (((1,), (1,)), ((), ())), preferred_element_type=jnp.float32
        )
        part = jnp.dot(
            flat_ref[:, term * rows : (term + 1) * rows], error, preferred_element_type=jnp.float32
        )
        total = part if total is None else total + part
    partial_ref[0] = total


def shards(record, target, offset, lag_steps):
    rows = record.shape[0]
    regions = target.shape[2]
    devices = lax.axis_size("region")
    begin_at = offset[0]
    window = lax.dynamic_slice_in_dim(record, begin_at, WIDE, 1)
    stacked, shifts = placed_early(window[:, :SAMPLES], lag_steps)
    scaled = stacked * jnp.bfloat16(1.0 / regions)
    flat = stacked[:, :, :SPAN].transpose(2, 0, 1).reshape(SPAN, TERMS * rows)
    turned = window.T
    gathered = lax.all_gather(turned, "region")
    blocks = regions // WIDTH
    if rows != WIDTH:
        gathered = (
            gathered.reshape(blocks, WIDTH // rows, WIDE, rows)
            .transpose(0, 2, 1, 3)
            .reshape(blocks, WIDE, WIDTH)
        )
    partials, own = pl.pallas_call(
        lambda *refs: block_kernel(SAMPLES / regions, *refs),
        grid=(blocks,),
        in_specs=[
            pl.BlockSpec((TERMS, rows, WIDE), lambda i: (0, 0, 0)),
            pl.BlockSpec((SPAN, TERMS * rows), lambda i: (0, 0)),
            pl.BlockSpec((1, WIDE, WIDTH), lambda i: (i, 0, 0)),
            pl.BlockSpec((TERMS, rows, WIDTH), lambda i: (0, 0, i)),
        ],
        out_specs=[
            pl.BlockSpec((1, SPAN, WIDTH), lambda i: (i, 0, 0)),
            pl.BlockSpec((TERMS, WIDE, rows), lambda i: (0, 0, 0)),
        ],
        out_shape=[
            jax.ShapeDtypeStruct((blocks, SPAN, WIDTH), jnp.float32),
            jax.ShapeDtypeStruct((TERMS, WIDE, rows), jnp.float32),
        ],
        compiler_params=pltpu.CompilerParams(vmem_limit_bytes=56 << 20),
        name="blocks",
    )(scaled, flat, gathered, target)
    if rows != WIDTH:
        partials = (
            partials.reshape(blocks, SPAN, WIDTH // rows, rows)
            .transpose(0, 2, 1, 3)
            .reshape(devices, SPAN, rows)
        )
    summed = lax.psum_scatter(partials, "region", scatter_dimension=0, tiled=True)[0]
    early = None
    for term in range(TERMS):
        part = lax.dynamic_slice(own[term], (shifts[term], 0), (SAMPLES, rows))
        early = part if early is None else early + part
    in_window = summed + jnp.pad(early, ((0, MAXLAG), (0, 0)))
    grad = jnp.zeros((record.shape[1], rows), jnp.float32)
    return lax.dynamic_update_slice(grad, in_window, (begin_at, 0)).T


def solution(mesh):
    placed = (
        P(("groups", "region"), None),
        P(None, ("groups", "region"), None),
        P("groups"),
        P("groups"),
    )
    return jax.shard_map(
        shards, mesh=mesh, in_specs=placed, out_specs=P(("groups", "region"), None), check_vma=False
    )
```

time: 1380 us -> 282 us (0.20)
  waiting for transfers between devices: 701 us -> 185 us
  local copies, waits for them, and re-layouts: 341 us -> 10.8 us
  matrix products: 130 us -> 0 us
  other arithmetic: 127 us -> 4.57 us
  Pallas kernels: 0 us -> 57 us
  starting transfers between devices: 55.9 us -> 0.04 us
  between operations: 6.93 us -> 24 us
    all_to_all x1 -> x0, waiting for transfers between devices: 568 us -> none  [shards(): lax.all_to_all(target, 'region', split_axis=2, concat_axis=2, tiled=True)]
    add x27 -> x1, local copies, waits for them, and re-layouts: 153 us -> 0.33 us  [shards(): in_window = summed + jnp.pad(early, ((0, MAXLAG), (0, 0)))]
    ppermute x17 -> x0, waiting for transfers between devices: 133 us -> none  [shifted(): return lax.ppermute(value, axis, pairs)]
    dot_general x76 -> x0, matrix products: 130 us -> none  [the longest x9 29 us: own_terms(): jnp.einsum('lrc,cs->lrs', back_err, other_early, preferred_element_type=j...]
    reduce_scatter x0 -> x1, waiting for transfers between devices: none -> 128 us  [shards(): lax.psum_scatter(partials, 'region', scatter_dimension=0, tiled=True)[0]]
    reshape x2 -> x1, local copies, waits for them, and re-layouts: 81 us -> 2.26 us  [shards(): flat = stacked[:, :, :SPAN].transpose(2, 0, 1).reshape(SPAN, TERMS * rows)]
    unnamed x17 -> x10, local copies, waits for them, and re-layouts: 58.8 us -> 1.44 us
    all_gather x0 -> x1, waiting for transfers between devices: none -> 57.3 us  [shards(): gathered = lax.all_gather(turned, 'region')]
  transfers between devices with their start and end apart: 18 -> 2, of which waited for: 9 -> 2; matrix products, arithmetic and copies ran while one was open for 30% -> 3% of each run, Pallas kernels for 0% -> 0%
where the time goes in v1:
time: 282 us
  waiting for transfers between devices  185 us (66%)
  Pallas kernels  57 us (20%)
  between operations  24 us (9%)
  local copies, waits for them, and re-layouts  10.8 us (4%)
  other arithmetic  4.57 us (2%)
    reduce_scatter x1, waiting for transfers between devices, shards(): lax.psum_scatter(partials, 'region', scatter_dimension=0, tiled=True)[0]  128 us
    all_gather x1, waiting for transfers between devices, shards(): gathered = lax.all_gather(turned, 'region')  57.3 us
    pallas_call x1, Pallas kernels, shards(): pl.pallas_call(lambda *refs: block_kernel(SAMPLES / regions, *refs), grid...  57 us
  transfers between devices with their start and end apart: 2, of which 2 were waited for; matrix products, arithmetic and copies ran while one was open for 3% of the time, Pallas kernels for 0%

profile of v1, /device:TPU:0, one launch (start us, length us, event | category | flops | bytes accessed | tf_op | source)
XLA Modules:
  0.0 281.5 jit_solution(9160691608727248560)
XLA Ops:
  6.5 0.0 copy-start
  6.5 0.0 copy-start.4
  6.5 0.0 all-gather.3.cloned.1.call-start
  7.3 0.4 copy-done
  7.6 0.3 dynamic-slice_bitcast_fusion
  7.9 0.9 copy.9
  8.8 0.0 all-gather.3.cloned.1.call-update
  8.9 0.0 reduce-scatter.2.cloned.1.call-start
  8.9 0.0 copy-done.4
  8.9 0.7 fusion.5
  13.4 0.2 constant_dynamic-slice_fusion
  13.6 0.9 fusion
  14.5 1.8 pad_maximum_fusion
  16.3 2.3 copy.11.refs_1_
  18.5 57.3 %all-gather.3.cloned.1.call-done = bf16[6400,512]{1,0:T(8,128)(2,1)} async-done(((bf16[400,512]{1,0:T(8,128)(2,1)}), bf16[6400,512]{1,0:T(8,128)(2,1)}) %all-gather.3.cloned.1.call-update) | async-done | bytes 6553616 | tf_op jit(solution)/shard_map/all_gather | solution.py:59
  75.8 57.0 %blocks.1 = (f32[16,392,512]{2,1,0:T(8,128)}, f32[4,400,512]{2,1,0:T(8,128)}) custom-call(bf16[4,512,400]{2,1,0:T(8,128)(2,1)} %get-tuple-element.13.refs_0_, bf16[392,2048]{1,0:T(8,128)(2,1)} %copy.11.refs_1_, bf16[16,400,512]{2,1,0:T(8,128)(2,1)} %bitcast.28, bf16[4,512,8192]{2,1,0:T(8,128)(2,1)} %refs_3_.1), custom_call_target="tpu_custom_call" | custom-call | tf_op jit(solution)/shard_map/blocks/pallas_call | solution.py:67
  132.7 0.0 copy-start.2
  132.7 0.0 reduce-scatter.2.cloned.1.call-update
  138.8 0.0 copy-done.2
  138.8 0.2 fusion.4
  139.0 1.3 add_bitcast_fusion
  140.3 127.8 %reduce-scatter.2.cloned.1.call-done = f32[1,392,512]{2,1,0:T(8,128)} async-done(((f32[16,392,512]{2,1,0:T(8,128)}), f32[1,392,512]{2,1,0:T(8,128)}) %reduce-scatter.2.cloned.1.call-update) | async-done | bytes 802832 | tf_op jit(solution)/shard_map/reduce_scatter | solution.py:93
  268.1 1.5 bitcast_add_fusion
  269.6 0.0 copy-start.1
  269.6 0.3 copy.10
  270.0 0.1 broadcast_in_dim.3
  270.1 3.5 %dynamic_update_slice.3 = f32[640,512]{0,1:T(8,128)S(1)} dynamic-update-slice(f32[640,512]{0,1:T(8,128)S(1)} %broadcast_in_dim.3, f32[392,512]{0,1:T(8,128)S(1)} %copy.10, s32[]{:T(128)S(6)} %select_n.22, s32[]{:T(128)} %constant.16.clone.1) | dynamic-update-slice | bytes 1605636 | tf_op jit(solution)/shard_map/dynamic_update_slice | solution.py:100
  273.6 0.0 copy-start.3
  273.6 1.0 copy-done.3
  274.7 0.0 copy-done.1
Async XLA Ops:
  6.5 1.1 copy-start
  6.5 2.4 copy-start.4
  6.5 69.2 %all-gather.3.cloned.1.call-start = ((), (), s32[]{:S(2)}) async-start(), calls=%async_computation.2 | async-start | bytes 6963200 | tf_op jit(solution)/shard_map/all_gather | solution.py:59
  8.9 259.2 %reduce-scatter.2.cloned.1.call-start = ((), (), s32[]{:S(2)}) async-start(), calls=%async_computation.1 | async-start | bytes 13647872 | tf_op jit(solution)/shard_map/reduce_scatter | solution.py:93
  132.7 6.0 %copy-start.2 = (f32[4,400,512]{2,1,0:T(8,128)S(1)}, f32[4,400,512]{2,1,0:T(8,128)}, u32[]{:S(2)}) copy-start(f32[4,400,512]{2,1,0:T(8,128)} %get-tuple-element.8) | copy-start | bytes 9830404
  269.6 5.1 %copy-start.1 = (bf16[512,640]{1,0:T(8,128)(2,1)S(1)}, bf16[512,640]{1,0:T(8,128)(2,1)}, u32[]{:S(2)}) copy-start(bf16[512,640]{1,0:T(8,128)(2,1)} %param.4) | copy-start | bytes 1966084
  273.6 1.1 copy-start.3
Sparse Core Ops, SparseCore 0:
  9.6 66.0 all-gather.2
  132.9 135.1 reduce-scatter.1

commit v2 on v1

--- a/solution.py
+++ b/solution.py
@@ -44,6 +44,235 @@
         )
         total = part if total is None else total + part
     partial_ref[0] = total
+
+
+def ring_place(index, count):
+    chips = count // 4
+    core = lax.rem(index, 2)
+    low = lax.rem(lax.div(index, 2), 2)
+    high = lax.div(index, 4)
+    return 2 * (high + low * (2 * chips - 1 - 2 * high)) + core
+
+
+def ring_index(place, count):
+    chips = count // 4
+    chip = lax.div(place, 2)
+    low = lax.div(chip, chips)
+    high = chip + low * (2 * chips - 1 - 2 * chip)
+    return 4 * high + 2 * low + lax.rem(place, 2)
+
+
+def ring_kernel(
+    count,
+    weight,
+    scaled_ref,
+    flat_ref,
+    turned_ref,
+    target_ref,
+    summed_ref,
+    own_ref,
+    windows,
+    sums,
+    tiles,
+    local_ref,
+    tile_sem,
+    window_send,
+    window_recv,
+    sum_send,
+    sum_recv,
+):
+    rows = target_ref.shape[1]
+    half = rows // 2
+    group = lax.axis_index("groups")
+    place = ring_place(lax.axis_index("region"), count)
+    after = ring_index(lax.rem(place + 1, count), count)
+    before = ring_index(lax.rem(place + count - 1, count), count)
+    nexts = ((group, after), (group, before))
+
+    def window_copy(step, side):
+        return pltpu.make_async_remote_copy(
+            src_ref=windows.at[step, side],
+            dst_ref=windows.at[step + 1, side],
+            send_sem=window_send.at[step, side],
+            recv_sem=window_recv.at[step + 1, side],
+            device_id=nexts[side],
+            device_id_type=pl.DeviceIdType.MESH,
+        )
+
+    def sum_copy(step, side):
+        return pltpu.make_async_remote_copy(
+            src_ref=sums.at[step, side],
+            dst_ref=sums.at[step + 1, side],
+            send_sem=sum_send.at[step, side],
+            recv_sem=sum_recv.at[step + 1, side],
+            device_id=nexts[side],
+            device_id_type=pl.DeviceIdType.MESH,
+        )
+
+    def tile_copy(step, side):
+        moved = (count - step, step)[side]
+        block = ring_index(lax.rem(place + moved, count), count)
+        column = pl.multiple_of(block * rows + side * half, half)
+        slot = lax.rem(step, 2)
+        return pltpu.make_async_copy(
+            target_ref.at[:, :, pl.ds(column, half)],
+            tiles.at[slot, side],
+            tile_sem.at[slot, side],
+        )
+
+    for side in range(2):
+        tile_copy(0, side).start()
+    windows[0] = turned_ref[...]
+    own_ref[...] = jnp.zeros_like(own_ref)
+
+    barrier = pltpu.get_barrier_semaphore()
+    for side in range(2):
+        pl.semaphore_signal(
+            barrier, inc=1, device_id=nexts[side], device_id_type=pl.DeviceIdType.MESH
+        )
+    pl.semaphore_wait(barrier, 2)
+    for side in range(2):
+        window_copy(0, side).start()
+
+    def visit(step, carry):
+        @pl.when(step < count - 1)
+        def _():
+            for side in range(2):
+                tile_copy(step + 1, side).start()
+
+        for side in range(2):
+            tile_copy(step, side).wait()
+        slot = lax.rem(step, 2)
+        window = jnp.concatenate([windows[step, 0], windows[step, 1]], axis=1)
+        total = None
+        for term in range(TERMS):
+            tile = jnp.concatenate([tiles[slot, 0, term], tiles[slot, 1, term]], axis=1)
+            cov = jnp.dot(scaled_ref[term], window, preferred_element_type=jnp.float32)
+            error = (cov - weight * tile.astype(jnp.float32)).astype(jnp.bfloat16)
+            own_ref[term] += lax.dot_general(
+                window, error, (((1,), (1,)), ((), ())), preferred_element_type=jnp.float32
+            )
+            part = jnp.dot(
+                flat_ref[:, term * rows : (term + 1) * rows],
+                error,
+                preferred_element_type=jnp.float32,
+            )
+            total = part if total is None else total + part
+        for side in range(2):
+            local_ref[side] = total[:, side * half : (side + 1) * half]
+
+        @pl.when(step < count - 1)
+        def _():
+            for side in range(2):
+                window_copy(step, side).wait_recv()
+
+        @pl.when(step < count - 2)
+        def _():
+            for side in range(2):
+                window_copy(step + 1, side).start()
+
+        @pl.when(step <= 1)
+        def _():
+            sums[step] = local_ref[...]
+
+        @pl.when(step > 1)
+        def _():
+            for side in range(2):
+                sum_copy(step - 1, side).wait_recv()
+                sums[step, side] += local_ref[side]
+
+        @pl.when(step > 0)
+        def _():
+            for side in range(2):
+                sum_copy(step, side).start()
+
+        return carry
+
+    lax.fori_loop(0, count, visit, 0)
+    for side in range(2):
+        sum_copy(count - 1, side).wait_recv()
+        summed_ref[:, side * half : (side + 1) * half] = sums[count, side] + sums[0, side]
+
+    def drain(step, carry):
+        for side in range(2):
+            window_copy(step, side).wait_send()
+            sum_copy(step + 1, side).wait_send()
+        return carry
+
+    lax.fori_loop(0, count - 1, drain, 0)
+
+
+def ring_call(count, regions, scaled, flat, turned, target):
+    rows = target.shape[1]
+    half = rows // 2
+    work = 6 * TERMS * rows * regions * SPAN
+    dma = pltpu.SemaphoreType.DMA
+    return pl.pallas_call(
+        lambda *refs: ring_kernel(count, SAMPLES / regions, *refs),
+        in_specs=[pl.BlockSpec(memory_space=pltpu.VMEM)] * 3
+        + [pl.BlockSpec(memory_space=pl.ANY)],
+        out_specs=[pl.BlockSpec(memory_space=pltpu.VMEM)] * 2,
+        out_shape=[
+            jax.ShapeDtypeStruct((SPAN, rows), jnp.float32),
+            jax.ShapeDtypeStruct((TERMS, WIDE, rows), jnp.float32),
+        ],
+        scratch_shapes=[
+            pltpu.VMEM((count, 2, WIDE, half), jnp.bfloat16),
+            pltpu.VMEM((count + 1, 2, SPAN, half), jnp.float32),
+            pltpu.VMEM((2, 2, TERMS, rows, half), jnp.bfloat16),
+            pltpu.VMEM((2, SPAN, half), jnp.float32),
+            dma((2, 2)),
+            dma((count, 2)),
+            dma((count, 2)),
+            dma((count + 1, 2)),
+            dma((count + 1, 2)),
+        ],
+        compiler_params=pltpu.CompilerParams(
+            collective_id=0, has_side_effects=True, vmem_limit_bytes=58 << 20
+        ),
+        cost_estimate=pl.CostEstimate(flops=work, bytes_accessed=40 << 20, transcendentals=0),
+        name="ring",
+    )(scaled, flat, turned, target)
+
+
+def gather_call(regions, devices, scaled, flat, turned, target):
+    rows = target.shape[1]
+    gathered = lax.all_gather(turned, "region")
+    blocks = regions // WIDTH
+    if rows != WIDTH:
+        gathered = (
+            gathered.reshape(blocks, WIDTH // rows, WIDE, rows)
+            .transpose(0, 2, 1, 3)
+            .reshape(blocks, WIDE, WIDTH)
+        )
+    partials, own = pl.pallas_call(
+        lambda *refs: block_kernel(SAMPLES / regions, *refs),
+        grid=(blocks,),
+        in_specs=[
+            pl.BlockSpec((TERMS, rows, WIDE), lambda i: (0, 0, 0)),
+            pl.BlockSpec((SPAN, TERMS * rows), lambda i: (0, 0)),
+            pl.BlockSpec((1, WIDE, WIDTH), lambda i: (i, 0, 0)),
+            pl.BlockSpec((TERMS, rows, WIDTH), lambda i: (0, 0, i)),
+        ],
+        out_specs=[
+            pl.BlockSpec((1, SPAN, WIDTH), lambda i: (i, 0, 0)),
+            pl.BlockSpec((TERMS, WIDE, rows), lambda i: (0, 0, 0)),
+        ],
+        out_shape=[
+            jax.ShapeDtypeStruct((blocks, SPAN, WIDTH), jnp.float32),
+            jax.ShapeDtypeStruct((TERMS, WIDE, rows), jnp.float32),
+        ],
+        compiler_params=pltpu.CompilerParams(vmem_limit_bytes=56 << 20),
+        name="blocks",
+    )(scaled, flat, gathered, target)
+    if rows != WIDTH:
+        partials = (
+            partials.reshape(blocks, SPAN, WIDTH // rows, rows)
+            .transpose(0, 2, 1, 3)
+            .reshape(devices, SPAN, rows)
+        )
+    summed = lax.psum_scatter(partials, "region", scatter_dimension=0, tiled=True)[0]
+    return summed, own
 
 
 def shards(record, target, offset, lag_steps):
@@ -56,41 +285,11 @@
     scaled = stacked * jnp.bfloat16(1.0 / regions)
     flat = stacked[:, :, :SPAN].transpose(2, 0, 1).reshape(SPAN, TERMS * rows)
     turned = window.T
-    gathered = lax.all_gather(turned, "region")
-    blocks = regions // WIDTH
-    if rows != WIDTH:
-        gathered = (
-            gathered.reshape(blocks, WIDTH // rows, WIDE, rows)
-            .transpose(0, 2, 1, 3)
-            .reshape(blocks, WIDE, WIDTH)
-        )
-    partials, own = pl.pallas_call(
-        lambda *refs: block_kernel(SAMPLES / regions, *refs),
-        grid=(blocks,),
-        in_specs=[
-            pl.BlockSpec((TERMS, rows, WIDE), lambda i: (0, 0, 0)),
-            pl.BlockSpec((SPAN, TERMS * rows), lambda i: (0, 0)),
-            pl.BlockSpec((1, WIDE, WIDTH), lambda i: (i, 0, 0)),
-            pl.BlockSpec((TERMS, rows, WIDTH), lambda i: (0, 0, i)),
-        ],
-        out_specs=[
-            pl.BlockSpec((1, SPAN, WIDTH), lambda i: (i, 0, 0)),
-            pl.BlockSpec((TERMS, WIDE, rows), lambda i: (0, 0, 0)),
-        ],
-        out_shape=[
-            jax.ShapeDtypeStruct((blocks, SPAN, WIDTH), jnp.float32),
-            jax.ShapeDtypeStruct((TERMS, WIDE, rows), jnp.float32),
-        ],
-        compiler_params=pltpu.CompilerParams(vmem_limit_bytes=56 << 20),
-        name="blocks",
-    )(scaled, flat, gathered, target)
-    if rows != WIDTH:
-        partials = (
-            partials.reshape(blocks, SPAN, WIDTH // rows, rows)
-            .transpose(0, 2, 1, 3)
-            .reshape(devices, SPAN, rows)
-        )
-    summed = lax.psum_scatter(partials, "region", scatter_dimension=0, tiled=True)[0]
+    if rows == WIDTH:
+        halves = turned.reshape(WIDE, 2, rows // 2).transpose(1, 0, 2)
+        summed, own = ring_call(devices, regions, scaled, flat, halves, target)
+    else:
+        summed, own = gather_call(regions, devices, scaled, flat, turned, target)
     early = None
     for term in range(TERMS):
         part = lax.dynamic_slice(own[term], (shifts[term], 0), (SAMPLES, rows))

time: 282 us -> 146 us (0.52)
  waiting for transfers between devices: 185 us -> 0 us
  Pallas kernels: 57 us -> 119 us
  between operations: 24 us -> 10.7 us
    reduce_scatter x1 -> x0, waiting for transfers between devices: 128 us -> none  [shards(): lax.psum_scatter(partials, 'region', scatter_dimension=0, tiled=True)[0]]
    pallas_call x1, Pallas kernels: 57 us -> 119 us  [ring_call(): pl.pallas_call(lambda *refs: ring_kernel(count, SAMPLES / regions, *refs)...]
    all_gather x1 -> x0, waiting for transfers between devices: 57.3 us -> none  [shards(): gathered = lax.all_gather(turned, 'region')]
  transfers between devices with their start and end apart: 2 -> 0, of which waited for: 2 -> 0; matrix products, arithmetic and copies ran while one was open for 3% -> 0% of each run, Pallas kernels for 0% -> 0%
where the time goes in v2:
time: 146 us
  Pallas kernels  119 us (82%)
  local copies, waits for them, and re-layouts  12.9 us (9%)
  between operations  10.7 us (7%)
  other arithmetic  3.56 us (2%)
    pallas_call x1, Pallas kernels, ring_call(): pl.pallas_call(lambda *refs: ring_kernel(count, SAMPLES / regions, *refs)...  119 us
    dynamic_update_slice x1, local copies, waits for them, and re-layouts, shards(): return lax.dynamic_update_slice(grad, in_window, (begin_at, 0)).T  3.55 us

profile of v2, /device:TPU:0, one launch (start us, length us, event | category | flops | bytes accessed | tf_op | source)
XLA Modules:
  0.0 145.7 jit_solution(8987274790835110411)
XLA Ops:
  0.0 0.0 copy-start
  0.0 1.4 fusion.5
  6.1 0.0 copy-done
  6.1 0.2 constant_dynamic-slice_fusion
  6.3 0.9 fusion
  7.2 1.8 %pad_maximum_fusion = (bf16[4,512,400]{2,1,0:T(8,128)(2,1)S(1)}, bf16[4,512,400]{2,1,0:T(8,128)(2,1)}) fusion(bf16[1,512,400]{2,1,0:T(8,128)(2,1)S(1)} %get-tuple-element.17, bf16[1,512,400]{2,1,0:T(8,128)(2,1)S(1)} %get-tuple-element.16, bf16[1,512,400]{2,1,0:T(8,128)(2,1)S(1)} %get-tuple-element.15, bf16[1,512,400]{2,1,0:T(8,128)(2,1)S(1)} %get-tuple-element.14), kind=kLoop, calls=%fused_computation | loop fusion | flops 3276800 | bytes 4915200 | tf_op jit(solution)/shard_map/stack | solution.py:24
  9.0 2.3 %copy.11.refs_1_ = bf16[392,2048]{1,0:T(8,128)(2,1)} copy(bf16[392,2048]{0,1:T(8,128)(2,1)S(1)} %bitcast.26) | data formatting | bytes 3211264 | tf_op jit(solution)/shard_map/reshape | solution.py:286
  11.3 0.3 constant_dynamic-slice_fusion.1
  11.5 1.0 copy.9
  12.5 118.5 %ring.1 = (f32[392,512]{1,0:T(8,128)}, f32[4,400,512]{2,1,0:T(8,128)}) custom-call(bf16[4,512,400]{2,1,0:T(8,128)(2,1)} %get-tuple-element.13.refs_0_, bf16[392,2048]{1,0:T(8,128)(2,1)} %copy.11.refs_1_, bf16[2,400,256]{2,1,0:T(8,128)(2,1)} %bitcast.28, bf16[4,512,8192]{2,1,0:T(8,128)(2,1)} %refs_3_.1), custom_call_target="tpu_custom_call" | custom-call | flops 39460012032 | bytes 41943040 | tf_op jit(solution)/shard_map/ring/pallas_call | solution.py:210
  131.0 1.9 %fusion.4 = (f32[1,400,512]{2,1,0:T(8,128)S(1)}, f32[1,400,512]{2,1,0:T(8,128)S(1)}, f32[1,400,512]{2,1,0:T(8,128)S(1)}) fusion(f32[4,400,512]{2,1,0:T(8,128)} %get-tuple-element.8), kind=kLoop, calls=%fused_computation.14 | loop fusion | bytes 4915200 | tf_op jit(solution)/shard_map/slice | solution.py:295
  138.9 0.0 copy-start.2
  138.9 1.6 %add_bitcast_fusion = f32[384,512]{1,0:T(8,128)S(1)} fusion(f32[1,400,512]{2,1,0:T(8,128)S(1)} %get-tuple-element.10, s32[]{:T(128)S(6)} %select_n.28, f32[1,400,512]{2,1,0:T(8,128)S(1)} %get-tuple-element.11, s32[]{:T(128)S(6)} %select_n.27, f32[1,400,512]{2,1,0:T(8,128)S(1)} %get-tuple-element.9, s32[]{:T(128)S(6)} %select_n.26, ...), kind=kLoop, calls=%fused_computation.3 | loop fusion | flops 589824 | bytes 3932172 | tf_op jit(solution)/shard_map/add | solution.py:296
  140.5 0.0 copy-done.2
  140.5 0.1 pad_add_fusion
  140.7 0.3 copy.10
  141.0 0.1 broadcast_in_dim.3
  141.1 3.5 %dynamic_update_slice.3 = f32[640,512]{0,1:T(8,128)S(1)} dynamic-update-slice(f32[640,512]{0,1:T(8,128)S(1)} %broadcast_in_dim.3, f32[392,512]{0,1:T(8,128)S(1)} %copy.10, s32[]{:T(128)S(6)} %select_n.22, s32[]{:T(128)} %constant.16.clone.1) | dynamic-update-slice | bytes 1605636 | tf_op jit(solution)/shard_map/dynamic_update_slice | solution.py:299
  144.6 0.0 copy-start.1
  144.7 1.0 copy-done.1
Async XLA Ops:
  0.0 6.1 %copy-start = (bf16[512,640]{1,0:T(8,128)(2,1)S(1)}, bf16[512,640]{1,0:T(8,128)(2,1)}, u32[]{:S(2)}) copy-start(bf16[512,640]{1,0:T(8,128)(2,1)} %param.4) | copy-start | bytes 1966084
  138.9 1.6 %copy-start.2 = (f32[392,512]{1,0:T(8,128)S(1)}, f32[392,512]{1,0:T(8,128)}, u32[]{:S(2)}) copy-start(f32[392,512]{1,0:T(8,128)} %get-tuple-element.7) | copy-start | bytes 2408452
  144.6 1.1 copy-start.1

commit v3 on v2

--- a/solution.py
+++ b/solution.py
@@ -12,6 +12,7 @@
 WIDE = 400
 SPAN = SAMPLES + MAXLAG
 WIDTH = 512
+CHUNKS = ((0, 104), (104, 96), (200, 96), (296, 96))
 
 
 def placed_early(early, lag_steps):
@@ -99,12 +100,13 @@
             device_id_type=pl.DeviceIdType.MESH,
         )
 
-    def sum_copy(step, side):
+    def sum_copy(step, side, chunk):
+        lines = pl.ds(*CHUNKS[chunk])
         return pltpu.make_async_remote_copy(
-            src_ref=sums.at[step, side],
-            dst_ref=sums.at[step + 1, side],
-            send_sem=sum_send.at[step, side],
-            recv_sem=sum_recv.at[step + 1, side],
+            src_ref=sums.at[step, side, lines],
+            dst_ref=sums.at[step + 1, side, lines],
+            send_sem=sum_send.at[step, side, chunk],
+            recv_sem=sum_recv.at[step + 1, side, chunk],
             device_id=nexts[side],
             device_id_type=pl.DeviceIdType.MESH,
         )
@@ -161,6 +163,25 @@
         for side in range(2):
             local_ref[side] = total[:, side * half : (side + 1) * half]
 
+        @pl.when(step <= 1)
+        def _():
+            sums[step] = local_ref[...]
+
+        @pl.when(step == 1)
+        def _():
+            for chunk in range(len(CHUNKS)):
+                for side in range(2):
+                    sum_copy(step, side, chunk).start()
+
+        @pl.when(step > 1)
+        def _():
+            for chunk, (first, size) in enumerate(CHUNKS):
+                lines = pl.ds(first, size)
+                for side in range(2):
+                    sum_copy(step - 1, side, chunk).wait_recv()
+                    sums[step, side, lines] += local_ref[side, lines]
+                    sum_copy(step, side, chunk).start()
+
         @pl.when(step < count - 1)
         def _():
             for side in range(2):
@@ -171,32 +192,19 @@
             for side in range(2):
                 window_copy(step + 1, side).start()
 
-        @pl.when(step <= 1)
-        def _():
-            sums[step] = local_ref[...]
-
-        @pl.when(step > 1)
-        def _():
-            for side in range(2):
-                sum_copy(step - 1, side).wait_recv()
-                sums[step, side] += local_ref[side]
-
-        @pl.when(step > 0)
-        def _():
-            for side in range(2):
-                sum_copy(step, side).start()
-
         return carry
 
     lax.fori_loop(0, count, visit, 0)
     for side in range(2):
-        sum_copy(count - 1, side).wait_recv()
+        for chunk in range(len(CHUNKS)):
+            sum_copy(count - 1, side, chunk).wait_recv()
         summed_ref[:, side * half : (side + 1) * half] = sums[count, side] + sums[0, side]
 
     def drain(step, carry):
         for side in range(2):
             window_copy(step, side).wait_send()
-            sum_copy(step + 1, side).wait_send()
+            for chunk in range(len(CHUNKS)):
+                sum_copy(step + 1, side, chunk).wait_send()
         return carry
 
     lax.fori_loop(0, count - 1, drain, 0)
@@ -224,8 +232,8 @@
             dma((2, 2)),
             dma((count, 2)),
             dma((count, 2)),
-            dma((count + 1, 2)),
-            dma((count + 1, 2)),
+            dma((count + 1, 2, len(CHUNKS))),
+            dma((count + 1, 2, len(CHUNKS))),
         ],
         compiler_params=pltpu.CompilerParams(
             collective_id=0, has_side_effects=True, vmem_limit_bytes=58 << 20
@@ -233,6 +241,72 @@
         cost_estimate=pl.CostEstimate(flops=work, bytes_accessed=40 << 20, transcendentals=0),
         name="ring",
     )(scaled, flat, turned, target)
+
+
+def prepare_kernel(scale, offset_ref, lag_ref, record_ref, scaled_ref, flat_ref, turned_ref):
+    rows, length = record_ref.shape
+    half = rows // 2
+    back = lax.rem(length - offset_ref[0], length)
+    window = pltpu.roll(record_ref[...].astype(jnp.float32), back, 1)[:, :WIDTH]
+    turned = window.T
+    for side in range(2):
+        turned_ref[side] = turned[:WIDE, side * half : (side + 1) * half].astype(jnp.bfloat16)
+    inside = lax.broadcasted_iota(jnp.int32, window.shape, 1) < SAMPLES
+    early = jnp.where(inside, window * scale, 0.0)
+    inside = lax.broadcasted_iota(jnp.int32, turned.shape, 0) < SAMPLES
+    early_turned = jnp.where(inside, turned, 0.0)
+    for term in range(TERMS):
+        shifted, shifted_turned = early, early_turned
+        if term:
+            shifted = pltpu.roll(early, lag_ref[term - 1], 1)
+            shifted_turned = pltpu.roll(early_turned, lag_ref[term - 1], 0)
+        scaled_ref[term] = shifted[:, :WIDE].astype(jnp.bfloat16)
+        flat_ref[:, term * rows : (term + 1) * rows] = shifted_turned[:SPAN].astype(jnp.bfloat16)
+
+
+def finish_kernel(offset_ref, lag_ref, summed_ref, own_ref, grad_ref):
+    rows, length = grad_ref.shape
+    early = own_ref[0, :SAMPLES, :]
+    for term in range(1, TERMS):
+        early = early + pltpu.roll(own_ref[term], WIDE - lag_ref[term - 1], 0)[:SAMPLES]
+    padded = jnp.concatenate(
+        [
+            summed_ref[:SAMPLES] + early,
+            summed_ref[SAMPLES:],
+            jnp.zeros((length - SPAN, rows), jnp.float32),
+        ],
+        axis=0,
+    )
+    grad_ref[...] = pltpu.roll(padded.T, offset_ref[0], 1)
+
+
+def ring_shards(record, target, offset, lag_steps):
+    rows, length = record.shape
+    regions = target.shape[2]
+    vmem = pl.BlockSpec(memory_space=pltpu.VMEM)
+    smem = pl.BlockSpec(memory_space=pltpu.SMEM)
+    scaled, flat, turned = pl.pallas_call(
+        lambda *refs: prepare_kernel(1.0 / regions, *refs),
+        in_specs=[smem, smem, vmem],
+        out_specs=[vmem] * 3,
+        out_shape=[
+            jax.ShapeDtypeStruct((TERMS, rows, WIDE), jnp.bfloat16),
+            jax.ShapeDtypeStruct((SPAN, TERMS * rows), jnp.bfloat16),
+            jax.ShapeDtypeStruct((2, WIDE, rows // 2), jnp.bfloat16),
+        ],
+        compiler_params=pltpu.CompilerParams(vmem_limit_bytes=60 << 20),
+        name="prepare",
+    )(offset, lag_steps, record)
+    devices = lax.axis_size("region")
+    summed, own = ring_call(devices, regions, scaled, flat, turned, target)
+    return pl.pallas_call(
+        finish_kernel,
+        in_specs=[smem, smem, vmem, vmem],
+        out_specs=vmem,
+        out_shape=jax.ShapeDtypeStruct((rows, length), jnp.float32),
+        compiler_params=pltpu.CompilerParams(vmem_limit_bytes=60 << 20),
+        name="finish",
+    )(offset, lag_steps, summed, own)
 
 
 def gather_call(regions, devices, scaled, flat, turned, target):
@@ -277,6 +351,8 @@
 
 def shards(record, target, offset, lag_steps):
     rows = record.shape[0]
+    if rows == WIDTH:
+        return ring_shards(record, target, offset, lag_steps)
     regions = target.shape[2]
     devices = lax.axis_size("region")
     begin_at = offset[0]
@@ -285,11 +361,7 @@
     scaled = stacked * jnp.bfloat16(1.0 / regions)
     flat = stacked[:, :, :SPAN].transpose(2, 0, 1).reshape(SPAN, TERMS * rows)
     turned = window.T
-    if rows == WIDTH:
-        halves = turned.reshape(WIDE, 2, rows // 2).transpose(1, 0, 2)
-        summed, own = ring_call(devices, regions, scaled, flat, halves, target)
-    else:
-        summed, own = gather_call(regions, devices, scaled, flat, turned, target)
+    summed, own = gather_call(regions, devices, scaled, flat, turned, target)
     early = None
     for term in range(TERMS):
         part = lax.dynamic_slice(own[term], (shifts[term], 0), (SAMPLES, rows))

time: 146 us -> 126 us (0.86)
  local copies, waits for them, and re-layouts: 12.9 us -> 0 us
  between operations: 10.7 us -> 0.66 us
  Pallas kernels: 119 us -> 125 us
  other arithmetic: 3.56 us -> 0 us
    pallas_call x0 -> x2, Pallas kernels: none -> 11.4 us  [the longest x1 5.92 us: ring_shards(): pl.pallas_call(lambda *refs: prepare_kernel(1.0 / regions, *refs), in_spe...]
    pallas_call x1, Pallas kernels: 119 us -> 114 us  [ring_call(): pl.pallas_call(lambda *refs: ring_kernel(count, SAMPLES / regions, *refs)...]
    dynamic_update_slice x1 -> x0, local copies, waits for them, and re-layouts: 3.55 us -> none  [shards(): return lax.dynamic_update_slice(grad, in_window, (begin_at, 0)).T]
    slice x3 -> x0, local copies, waits for them, and re-layouts: 3.48 us -> none  [the longest x1 1.86 us: shards(): part = lax.dynamic_slice(own[term], (shifts[term], 0), (SAMPLES, rows))]
    reshape x2 -> x0, local copies, waits for them, and re-layouts: 3.24 us -> none  [the longest x1 2.28 us: shards(): flat = stacked[:, :, :SPAN].transpose(2, 0, 1).reshape(SPAN, TERMS * rows)]
    another operation x1 -> x0, other arithmetic: 1.82 us -> none  [placed_early(): return (jnp.stack(parts), shifts)]
    add x2 -> x0, other arithmetic: 1.74 us -> none  [the longest x1 1.6 us: shards(): early = part if early is None else early + part]
where the time goes in v3:
time: 126 us
  Pallas kernels  125 us (99%)
    pallas_call x1, Pallas kernels, ring_call(): pl.pallas_call(lambda *refs: ring_kernel(count, SAMPLES / regions, *refs)...  114 us
    pallas_call x1, Pallas kernels, ring_shards(): pl.pallas_call(lambda *refs: prepare_kernel(1.0 / regions, *refs), in_spe...  5.92 us
    pallas_call x1, Pallas kernels, ring_shards(): pl.pallas_call(finish_kernel, in_specs=[smem, smem, vmem, vmem], out_spec...  5.46 us

profile of v3, /device:TPU:0, one launch (start us, length us, event | category | flops | bytes accessed | tf_op | source)
XLA Modules:
  0.0 126.0 jit_solution(15276550509942061094)
XLA Ops:
  0.7 5.9 %prepare.1 = (bf16[4,512,400]{2,1,0:T(8,128)(2,1)}, bf16[392,2048]{1,0:T(8,128)(2,1)}, bf16[2,400,256]{2,1,0:T(8,128)(2,1)}) custom-call(s32[1]{0:T(128)S(6)} %copy.5.refs_0_.offset_ref, s32[3]{0:T(128)} %lag_ref.1, bf16[512,640]{1,0:T(8,128)(2,1)} %refs_2_.1), custom_call_target="tpu_custom_call" | custom-call | tf_op jit(solution)/shard_map/prepare/pallas_call | solution.py:288
  6.6 113.9 %ring.1 = (f32[392,512]{1,0:T(8,128)}, f32[4,400,512]{2,1,0:T(8,128)}) custom-call(bf16[4,512,400]{2,1,0:T(8,128)(2,1)} %get-tuple-element.10.refs_0_, bf16[392,2048]{1,0:T(8,128)(2,1)} %get-tuple-element.11.refs_1_, bf16[2,400,256]{2,1,0:T(8,128)(2,1)} %get-tuple-element.12.refs_2_, bf16[4,512,8192]{2,1,0:T(8,128)(2,1)} %refs_3_.1), custom_call_target="tpu_custom_call" | custom-call | flops 39460012032 | bytes 41943040 | tf_op jit(solution)/shard_map/ring/pallas_call | solution.py:218
  120.5 5.5 %finish.1 = f32[512,640]{1,0:T(8,128)} custom-call(s32[1]{0:T(128)S(6)} %copy.5.refs_0_.offset_ref, s32[3]{0:T(128)} %lag_ref.1, f32[392,512]{1,0:T(8,128)} %get-tuple-element.13.summed_ref, f32[4,400,512]{2,1,0:T(8,128)} %get-tuple-element.14.own_ref), custom_call_target="tpu_custom_call" | custom-call | tf_op jit(solution)/shard_map/finish/pallas_call | solution.py:302
